TPU v7x, 512 devices: a whole 4x4x16 slice. The times are simulated.
512 devices in a mesh: grid: 4 (over z_lo), gx: 16 (over x, y), gy: 8 (over z_hi, core).
Axes of the slice: x: 4, y: 4, z: 16 (z_hi: 4, z_lo: 4; z = z_hi * 4 + z_lo), core: 2. Of those that a mesh axis runs over, the one named last changes fastest.
Arguments:
- adjoint: float32 [4, 24, 512, 2048], P('grid', None, 'gx', 'gy'), may hold values from -6 to 6
- sea_mask: int32 [4, 512, 2048], P('grid', 'gx', 'gy'), may hold values 0 or 1
- diffusivity: float32 [4, 512, 2048], P('grid', 'gx', 'gy'), may hold values from 0.03 to 0.24
- aggregation: float32 [4, 512, 2048], P('grid', 'gx', 'gy'), may hold values from 0.02 to 0.3
- breakup: float32 [4, 512, 2048], P('grid', 'gx', 'gy'), may hold values from 0.02 to 0.3
- sponge: float32 [4, 512, 2048], P('grid', 'gx', 'gy'), may hold values from 0.05 to 0.6
- settling: float32 [4, 3], replicated, may hold values from 0.05 to 0.5
- partner_flip: int32 [3, 16, 8], replicated, may hold values from 0 to 1
- row_offset: int32 [3, 16, 8], replicated, may hold values from 0 to 16
- col_offset: int32 [3, 16, 8], replicated, may hold values from 0 to 128
Outputs:
- adjoint_out: float32 [4, 24, 512, 2048], P('grid', None, 'gx', 'gy')
Inputs may be any that keep to these rules, and one draw needn't show every extreme that they name: `partner_flip`: every child tile is paired with exactly one parent tile in its own tile column, in its own tile row or the row whose index differs in the lowest bit; a parent tile serves 0 to 6 child tiles. `row_offset`: the footprint lies inside the paired parent tile. `col_offset`: the footprint lies inside the paired parent tile.
All inputs are finite; a program needn't handle non-finite values. No bound on the sum of `sea_mask` on one device may be relied on, other than what follows from the above.
Results may differ from a plain program's by a relative error of at most 0.0001.
Values sent between devices are 32-bit elements; how exact they have to be, the bound alone decides.
A program may use at most 64 MiB of HBM per device.

v0:
```python
import jax
import jax.numpy as jnp
from jax import lax
from jax.sharding import PartitionSpec as P

NCLS = 3
LEV = 8
STEPS = 2
relaxation = 0.125


def partner(value, axis, distance):
    mask = 2**distance
    pairs = [(source, source ^ mask) for source in range(lax.axis_size(axis))]
    return lax.ppermute(value, axis, pairs)


def spread(block, axis, holder):
    block = jnp.where(lax.axis_index(axis) == holder, block, jnp.zeros_like(block))
    return lax.psum(block, axis)


def padded_2(shard, sides, width):
    for axis, dim in sides:
        size, length = (lax.axis_size(axis), shard.shape[dim])
        up = [(i, (i + 1) % size) for i in range(size - 1)]
        down = [(j, i) for i, j in up]
        last = lax.slice_in_dim(shard, length - width, length, axis=dim)
        leading = lax.slice_in_dim(shard, 0, width, axis=dim)
        before = lax.ppermute(last, axis, up)
        after = lax.ppermute(leading, axis, down)
        shard = jnp.concatenate([before, shard, after], axis=dim)
    return shard


def block_sums(values):
    shape = values.shape
    return values.reshape(shape[:-2] + (shape[-2] // 2, 2, shape[-1] // 2, 2)).sum(axis=(-3, -1))


def expand_cells(values):
    return jnp.repeat(jnp.repeat(values, 2, axis=-2), 2, axis=-1)


def floc_adjoint(values, aggregation, breakup):
    shape = values.shape
    split = values.reshape((shape[0], NCLS, LEV) + shape[2:])
    agg = aggregation[:, None]
    brk = breakup[:, None]
    first = split[:, 0]
    second = split[:, 1]
    third = split[:, 2]
    new_first = (1.0 - agg) * first + agg * second
    new_second = brk * first + (1.0 - agg - brk) * second + agg * third
    new_third = brk * second + (1.0 - brk) * third
    return jnp.stack([new_first, new_second, new_third], axis=1).reshape(shape)


def settle_adjoint(values, rates):
    shape = values.shape
    split = values.reshape((shape[0], NCLS, LEV) + shape[2:])
    below = jnp.concatenate([split[:, :, 1:], jnp.zeros_like(split[:, :, :1])], axis=2)
    speed = rates[:, :, None, None, None]
    return ((1.0 - speed) * split + speed * below).reshape(shape)


def local(
    adjoint,
    sea_mask,
    diffusivity,
    aggregation,
    breakup,
    sponge,
    settling,
    partner_flip,
    row_offset,
    col_offset,
):
    n_grid = lax.axis_size("grid")
    slots = n_grid - 1
    grid_index = lax.axis_index("grid")
    row_index = lax.axis_index("gx")
    col_index = lax.axis_index("gy")
    partner_row = jnp.bitwise_xor(row_index, 1)
    is_parent = grid_index == 0
    own_slot = jnp.maximum(grid_index - 1, 0)
    flips_here = partner_flip[:, row_index, col_index]
    flips_there = partner_flip[:, partner_row, col_index]
    tops_here = row_offset[:, row_index, col_index]
    lefts_here = col_offset[:, row_index, col_index]
    tops_there = row_offset[:, partner_row, col_index]
    lefts_there = col_offset[:, partner_row, col_index]
    keep_here = (flips_here == 0).astype(jnp.float32)
    take_there = (flips_there == 1).astype(jnp.float32)
    components = adjoint.shape[1]
    cells_r = adjoint.shape[2]
    cells_c = adjoint.shape[3]
    half_r = cells_r // 2
    half_c = cells_c // 2
    anchor = jnp.zeros((), jnp.int32)
    settle_rates = settling[grid_index][None]
    weights = sponge[0]
    wet_mask = sea_mask.astype(jnp.float32)[:, None]
    row_ids = lax.broadcasted_iota(jnp.int32, (cells_r, cells_c), 0)
    col_ids = lax.broadcasted_iota(jnp.int32, (cells_r, cells_c), 1)
    covered = jnp.zeros((cells_r, cells_c), jnp.float32)
    for slot in range(slots):
        for tops, lefts, flags in (
            (tops_here, lefts_here, keep_here),
            (tops_there, lefts_there, take_there),
        ):
            inside = (
                (row_ids >= tops[slot])
                & (row_ids < tops[slot] + half_r)
                & (col_ids >= lefts[slot])
                & (col_ids < lefts[slot] + half_c)
            )
            covered = covered + flags[slot] * inside.astype(jnp.float32)
    state = adjoint
    for step_number in range(STEPS):
        current = state[0]
        child_block = block_sums(weights * current)
        down_here = jnp.stack(
            [
                keep_here[slot]
                * lax.dynamic_slice(
                    current,
                    (anchor, tops_here[slot], lefts_here[slot]),
                    (components, half_r, half_c),
                )
                for slot in range(slots)
            ]
        )
        down_there = jnp.stack(
            [
                take_there[slot]
                * lax.dynamic_slice(
                    current,
                    (anchor, tops_there[slot], lefts_there[slot]),
                    (components, half_r, half_c),
                )
                for slot in range(slots)
            ]
        )
        gathered_up = lax.all_gather(child_block[None], "grid", axis=0, tiled=True)[1:]
        up_keep = keep_here[:, None, None, None] * gathered_up
        up_send = (1.0 - keep_here)[:, None, None, None] * gathered_up
        up_cross, down_cross = partner((up_send, down_there), "gx", 0)
        down_all = spread(down_here + down_cross, "grid", 0)
        from_parent = down_all[own_slot]
        child_new = (1.0 - weights) * current + relaxation / 4.0 * expand_cells(from_parent)
        gathered = jnp.zeros_like(current)
        for slot in range(slots):
            for tops, lefts, pieces in (
                (tops_here, lefts_here, up_keep),
                (tops_there, lefts_there, up_cross),
            ):
                existing = lax.dynamic_slice(
                    gathered, (anchor, tops[slot], lefts[slot]), (components, half_r, half_c)
                )
                gathered = lax.dynamic_update_slice(
                    gathered, existing + pieces[slot], (anchor, tops[slot], lefts[slot])
                )
        parent_new = (1.0 - relaxation * covered) * current + gathered
        state = jnp.where(is_parent, parent_new, child_new)[None]
        state = floc_adjoint(state, aggregation, breakup)
        state = settle_adjoint(state, settle_rates)
        wet = wet_mask * state
        flux = diffusivity[:, None] * wet
        padded = padded_2(flux, (("gx", 2), ("gy", 3)), 1)
        state = (
            wet
            + padded[:, :, :-2, 1:-1]
            + padded[:, :, 2:, 1:-1]
            + padded[:, :, 1:-1, :-2]
            + padded[:, :, 1:-1, 2:]
            - 4.0 * flux
        )
    return state


def solution(mesh):
    in_specs = (
        P("grid", None, "gx", "gy"),
        P("grid", "gx", "gy"),
        P("grid", "gx", "gy"),
        P("grid", "gx", "gy"),
        P("grid", "gx", "gy"),
        P("grid", "gx", "gy"),
        P(),
        P(),
        P(),
        P(),
    )
    out_specs = P("grid", None, "gx", "gy")
    return jax.shard_map(local, mesh=mesh, in_specs=in_specs, out_specs=out_specs, check_vma=False)
```

profile of v0, /device:TPU:25, one launch (start us, length us, event | category | flops | bytes accessed | tf_op | source)
XLA Modules:
  0.0 421.5 jit_solution(10322343063372970234)
XLA Ops:
  33.4 7.3 %dynamic-slice_multiply_fusion.11 = (f32[1,24,16,128]{3,2,1,0:T(8,128)}, f32[1,24,16,128]{3,2,1,0:T(8,128)S(1)}, f32[1,24,16,128]{3,2,1,0:T(8,128)}, f32[1,24,16...) fusion(f32[1,24,32,256]{3,2,1,0:T(8,128)} %param.10, s32[]{:T(128)S(6)} %select_n.61, ...), kind=kLoop, calls=%fused_computation.97 | loop fusion | flops 294912 | bytes 2359368 | tf_op jit(solution)/shard_map/mul | solution.py:125
  48.7 7.2 %multiply_reduce_fusion.1 = f32[24,16,128]{0,2,1:T(8,128)} fusion(f32[24,16,2,128,2]{0,4,3,2,1:T(2,128)} %bitcast.116, f32[16,2,128,2]{3,2,1,0:T(8,128)S(1)} %mul.540), kind=kLoop, calls=%fused_computation.1 | loop fusion | flops 344064 | bytes 1015808 | tf_op jit(solution)/shard_map/reduce_sum | solution.py:38
  57.4 17.7 %all-gather = f32[96,16,128]{2,1,0:T(8,128)S(1)} all-gather(f32[24,16,128]{2,1,0:T(8,128)S(1)} %copy.39), channel_id=2, replica_groups=mesh['grid'=4,'gx'=16,'gy'=8] {'grid'}, dimensions={0}, use_global_device_ids=true | all-gather | bytes 983040 | tf_op jit(solution)/shard_map/all_gather | solution.py:145
  100.4 9.0 %dynamic_update_slice.36 = f32[24,32,256]{2,1,0:T(8,128)} dynamic-update-slice(f32[24,32,256]{2,1,0:T(8,128)} %broadcast.563.clone, f32[24,16,128]{2,1,0:T(8,128)} %slice_bitcast_fusion.11, s32[]{:T(128)} %constant.55.clone.1, s32[]{:T(128)S(6)} %select_n.61, s32[]{:T(128)S(6)} %select_n.62) | dynamic-update-slice | bytes 393220 | tf_op jit(solution)/shard_map/dynamic_update_slice | solution.py:161
  116.5 9.0 %dynamic_update_slice.37 = f32[24,32,256]{2,1,0:T(8,128)} dynamic-update-slice(f32[24,32,256]{2,1,0:T(8,128)} %dynamic_update_slice.36, f32[24,16,128]{2,1,0:T(8,128)} %fusion.27, s32[]{:T(128)} %constant.55.clone.1, s32[]{:T(128)S(6)} %select_n.63, s32[]{:T(128)S(6)} %select_n.64) | dynamic-update-slice | bytes 393220 | tf_op jit(solution)/shard_map/dynamic_update_slice | solution.py:161
  127.3 8.4 %dynamic_update_slice.38 = f32[24,32,256]{2,1,0:T(8,128)} dynamic-update-slice(f32[24,32,256]{2,1,0:T(8,128)} %dynamic_update_slice.37, f32[24,16,128]{2,1,0:T(8,128)} %fusion.26, s32[]{:T(128)} %constant.55.clone.1, s32[]{:T(128)S(6)} %select_n.65, s32[]{:T(128)S(6)} %select_n.66) | dynamic-update-slice | bytes 393220 | tf_op jit(solution)/shard_map/dynamic_update_slice | solution.py:161
  137.7 9.0 %dynamic_update_slice.39 = f32[24,32,256]{2,1,0:T(8,128)} dynamic-update-slice(f32[24,32,256]{2,1,0:T(8,128)} %dynamic_update_slice.38, f32[24,16,128]{2,1,0:T(8,128)} %fusion.25, s32[]{:T(128)} %constant.55.clone.1, s32[]{:T(128)S(6)} %select_n.67, s32[]{:T(128)S(6)} %select_n.68) | dynamic-update-slice | bytes 393220 | tf_op jit(solution)/shard_map/dynamic_update_slice | solution.py:161
  148.5 9.0 %dynamic_update_slice.40 = f32[24,32,256]{2,1,0:T(8,128)} dynamic-update-slice(f32[24,32,256]{2,1,0:T(8,128)} %dynamic_update_slice.39, f32[24,16,128]{2,1,0:T(8,128)} %fusion.24, s32[]{:T(128)} %constant.55.clone.1, s32[]{:T(128)S(6)} %select_n.69, s32[]{:T(128)S(6)} %select_n.70) | dynamic-update-slice | bytes 393220 | tf_op jit(solution)/shard_map/dynamic_update_slice | solution.py:161
  158.8 9.0 %dynamic_update_slice.41 = f32[24,32,256]{2,1,0:T(8,128)} dynamic-update-slice(f32[24,32,256]{2,1,0:T(8,128)} %dynamic_update_slice.40, f32[24,16,128]{2,1,0:T(8,128)S(1)} %fusion.23, s32[]{:T(128)} %constant.55.clone.1, s32[]{:T(128)S(6)} %select_n.71, s32[]{:T(128)S(6)} %select_n.72) | dynamic-update-slice | bytes 393220 | tf_op jit(solution)/shard_map/dynamic_update_slice | solution.py:161
  167.8 13.7 %all-reduce.5.cloned.1.call-done = f32[3,24,16,128]{3,2,1,0:T(8,128)} async-done(((f32[3,24,16,128]{3,2,1,0:T(8,128)}), f32[3,24,16,128]{3,2,1,0:T(8,128)}) %all-reduce.5.cloned.1.call-update) | async-done | bytes 589840 | tf_op jit(solution)/shard_map/psum | solution.py:20
  202.9 11.8 %collective-permute-start.4 = (f32[1,24,34,1]{3,2,1,0:T(8,128)S(1)}, f32[1,24,34,1]{3,2,1,0:T(8,128)S(1)}, u32[]{:S(2)}, u32[]{:S(2)}) collective-permute-start(f32[1,24,34,1]{3,2,1,0:T(8,128)S(1)} %get-tuple-element.11), channel_id=1, source_target_pairs={{0,1},{1,2},{2,3},{3,4},{4,5},{5,6},{6,7},{8,9},{9,10},{10,11},{11... | collective-permute-start | bytes 9800 | tf_op jit(solution)/shard_map/ppermute | solution.py:30
  220.7 23.0 %collective-permute-done.5 = f32[1,24,34,1]{3,2,1,0:T(8,128)S(1)} collective-permute-done((f32[1,24,34,1]{3,2,1,0:T(8,128)S(1)}, f32[1,24,34,1]{3,2,1,0:T(8,128)S(1)}, u32[]{:S(2)}, u32[]{:S(2)}) %collective-permute-start.5) | collective-permute-done | bytes 3296 | tf_op jit(solution)/shard_map/ppermute | solution.py:31
  244.5 5.0 %dynamic-slice_multiply_fusion.5 = (f32[1,24,16,128]{3,2,1,0:T(8,128)}, f32[1,24,16,128]{3,2,1,0:T(8,128)S(1)}, f32[1,24,16,128]{3,2,1,0:T(8,128)S(1)}, f32[1,24...) fusion(f32[1,24,32,256]{3,2,1,0:T(8,128)S(1)} %fusion.6, s32[]{:T(128)S(6)} %select_n.61, ...), kind=kLoop, calls=%fused_computation.90 | loop fusion | flops 294912 | bytes 2359368 | tf_op jit(solution)/shard_map/mul | solution.py:125
  254.9 7.2 %multiply_reduce_fusion = f32[24,16,128]{0,2,1:T(8,128)} fusion(f32[24,16,2,128,2]{0,4,3,2,1:T(2,128)} %bitcast.115, f32[16,2,128,2]{3,2,1,0:T(8,128)S(1)} %mul.540), kind=kLoop, calls=%fused_computation | loop fusion | flops 344064 | bytes 1015808 | tf_op jit(solution)/shard_map/reduce_sum | solution.py:38
  263.7 12.8 %all-gather.1 = f32[96,16,128]{2,1,0:T(8,128)S(1)} all-gather(f32[24,16,128]{2,1,0:T(8,128)S(1)} %copy.44), channel_id=3, replica_groups=mesh['grid'=4,'gx'=16,'gy'=8] {'grid'}, dimensions={0}, use_global_device_ids=true | all-gather | bytes 983040 | tf_op jit(solution)/shard_map/all_gather | solution.py:145
  281.0 7.9 %dynamic_update_slice.42 = f32[24,32,256]{2,1,0:T(8,128)S(1)} dynamic-update-slice(f32[24,32,256]{2,1,0:T(8,128)S(1)} %broadcast.563, f32[24,16,128]{2,1,0:T(8,128)S(1)} %slice_bitcast_fusion.5, s32[]{:T(128)} %constant.55.clone.1, s32[]{:T(128)S(6)} %select_n.61, s32[]{:T(128)S(6)} %select_n.62) | dynamic-update-slice | bytes 393220 | tf_op jit(solution)/shard_map/dynamic_update_slice | solution.py:161
  291.1 7.9 %dynamic_update_slice.43 = f32[24,32,256]{2,1,0:T(8,128)S(1)} dynamic-update-slice(f32[24,32,256]{2,1,0:T(8,128)S(1)} %dynamic_update_slice.42, f32[24,16,128]{2,1,0:T(8,128)S(1)} %fusion.22, s32[]{:T(128)} %constant.55.clone.1, s32[]{:T(128)S(6)} %select_n.63, s32[]{:T(128)S(6)} %select_n.64) | dynamic-update-slice | bytes 393220 | tf_op jit(solution)/shard_map/dynamic_update_slice | solution.py:161
  299.1 7.7 %dynamic_update_slice.44 = f32[24,32,256]{2,1,0:T(8,128)S(1)} dynamic-update-slice(f32[24,32,256]{2,1,0:T(8,128)S(1)} %dynamic_update_slice.43, f32[24,16,128]{2,1,0:T(8,128)S(1)} %fusion.21, s32[]{:T(128)} %constant.55.clone.1, s32[]{:T(128)S(6)} %select_n.65, s32[]{:T(128)S(6)} %select_n.66) | dynamic-update-slice | bytes 393220 | tf_op jit(solution)/shard_map/dynamic_update_slice | solution.py:161
  307.0 7.9 %dynamic_update_slice.45 = f32[24,32,256]{2,1,0:T(8,128)S(1)} dynamic-update-slice(f32[24,32,256]{2,1,0:T(8,128)S(1)} %dynamic_update_slice.44, f32[24,16,128]{2,1,0:T(8,128)S(1)} %fusion.20, s32[]{:T(128)} %constant.55.clone.1, s32[]{:T(128)S(6)} %select_n.67, s32[]{:T(128)S(6)} %select_n.68) | dynamic-update-slice | bytes 393220 | tf_op jit(solution)/shard_map/dynamic_update_slice | solution.py:161
  315.0 7.9 %dynamic_update_slice.46 = f32[24,32,256]{2,1,0:T(8,128)S(1)} dynamic-update-slice(f32[24,32,256]{2,1,0:T(8,128)S(1)} %dynamic_update_slice.45, f32[24,16,128]{2,1,0:T(8,128)S(1)} %fusion.19, s32[]{:T(128)} %constant.55.clone.1, s32[]{:T(128)S(6)} %select_n.69, s32[]{:T(128)S(6)} %select_n.70) | dynamic-update-slice | bytes 393220 | tf_op jit(solution)/shard_map/dynamic_update_slice | solution.py:161
  323.1 7.9 %dynamic_update_slice.47 = f32[24,32,256]{2,1,0:T(8,128)S(1)} dynamic-update-slice(f32[24,32,256]{2,1,0:T(8,128)S(1)} %dynamic_update_slice.46, f32[24,16,128]{2,1,0:T(8,128)S(1)} %fusion.18, s32[]{:T(128)} %constant.55.clone.1, s32[]{:T(128)S(6)} %select_n.71, s32[]{:T(128)S(6)} %select_n.72) | dynamic-update-slice | bytes 393220 | tf_op jit(solution)/shard_map/dynamic_update_slice | solution.py:161
  331.0 20.2 %all-reduce.7.cloned.1.call-done = f32[3,24,16,128]{3,2,1,0:T(8,128)} async-done(((f32[3,24,16,128]{3,2,1,0:T(8,128)}), f32[3,24,16,128]{3,2,1,0:T(8,128)}) %all-reduce.7.cloned.1.call-update) | async-done | bytes 589840 | tf_op jit(solution)/shard_map/psum | solution.py:20
  372.6 11.7 %collective-permute-start.10 = (f32[1,24,34,1]{3,2,1,0:T(8,128)S(1)}, f32[1,24,34,1]{3,2,1,0:T(8,128)S(1)}, u32[]{:S(2)}, u32[]{:S(2)}) collective-permute-start(f32[1,24,34,1]{3,2,1,0:T(8,128)S(1)} %get-tuple-element.9), channel_id=1, source_target_pairs={{0,1},{1,2},{2,3},{3,4},{4,5},{5,6},{6,7},{8,9},{9,10},{10,11},{11... | collective-permute-start | bytes 9800 | tf_op jit(solution)/shard_map/ppermute | solution.py:30
  390.2 22.8 %collective-permute-done.11 = f32[1,24,34,1]{3,2,1,0:T(8,128)S(1)} collective-permute-done((f32[1,24,34,1]{3,2,1,0:T(8,128)S(1)}, f32[1,24,34,1]{3,2,1,0:T(8,128)S(1)}, u32[]{:S(2)}, u32[]{:S(2)}) %collective-permute-start.11) | collective-permute-done | bytes 3296 | tf_op jit(solution)/shard_map/ppermute | solution.py:31
  (148 shorter events, 116.6 us)
Async XLA Ops:
  6.5 37.4 %copy-start = (f32[1,24,32,256]{3,2,1,0:T(8,128)S(1)}, f32[1,24,32,256]{3,2,1,0:T(8,128)}, u32[]{:S(2)}) copy-start(f32[1,24,32,256]{3,2,1,0:T(8,128)} %param.10) | copy-start | bytes 2359300
  6.5 175.0 %all-reduce.5.cloned.1.call-start = ((), (), s32[]{:S(2)}) async-start(), calls=%async_computation | async-start | bytes 1179648 | tf_op jit(solution)/shard_map/psum | solution.py:20
  33.4 13.2 %copy-start.15 = (f32[1,32,256]{2,1,0:T(8,128)S(1)}, f32[1,32,256]{2,1,0:T(8,128)}, u32[]{:S(2)}) copy-start(f32[1,32,256]{2,1,0:T(8,128)} %param.15) | copy-start | bytes 98308
  41.6 70.7 %collective-permute-start.1 = (f32[3,24,16,128]{3,2,1,0:T(8,128)}, f32[3,24,16,128]{3,2,1,0:T(8,128)}, u32[]{:S(2)}, u32[]{:S(2)}) collective-permute-start(f32[3,24,16,128]{3,2,1,0:T(8,128)} %pad_maximum_fusion.20), channel_id=1, source_target_pairs={{0,8},{8,0},{16,24},{24,16},{32,40},{40,32},{48,56},{56,48},{64,72... | collective-permute-start | bytes 1769480 | tf_op jit(solution)/shard_map/ppermute | solution.py:15
  76.2 38.4 %collective-permute-start = (f32[3,24,16,128]{3,2,1,0:T(8,128)}, f32[3,24,16,128]{3,2,1,0:T(8,128)}, u32[]{:S(2)}, u32[]{:S(2)}) collective-permute-start(f32[3,24,16,128]{3,2,1,0:T(8,128)} %get-tuple-element.37), channel_id=1, source_target_pairs={{0,8},{8,0},{16,24},{24,16},{32,40},{40,32},{48,56},{56,48},{64,72... | collective-permute-start | bytes 1769480 | tf_op jit(solution)/shard_map/ppermute | solution.py:15
  114.5 236.7 %all-reduce.7.cloned.1.call-start = ((), (), s32[]{:S(2)}) async-start(), calls=%async_computation.1 | async-start | bytes 1179648 | tf_op jit(solution)/shard_map/psum | solution.py:20
  184.2 6.4 %copy-start.3 = (f32[32,256]{1,0:T(8,128)S(1)}, f32[32,256]{1,0:T(8,128)}, u32[]{:S(2)}) copy-start(f32[32,256]{1,0:T(8,128)} %multiply_subtract_fusion) | copy-start | bytes 98308
  187.5 4.8 %copy-start.7 = (f32[1,32,256]{2,1,0:T(8,128)S(1)}, f32[1,32,256]{2,1,0:T(8,128)}, u32[]{:S(2)}) copy-start(f32[1,32,256]{2,1,0:T(8,128)} %param.14) | copy-start | bytes 98308
  187.5 4.8 %copy-start.9 = (f32[32,256]{1,0:T(8,128)S(1)}, f32[32,256]{1,0:T(8,128)}, u32[]{:S(2)}) copy-start(f32[32,256]{1,0:T(8,128)} %get-tuple-element.39) | copy-start | bytes 98308
  187.5 4.8 %copy-start.11 = (f32[32,256]{1,0:T(8,128)S(1)}, f32[32,256]{1,0:T(8,128)}, u32[]{:S(2)}) copy-start(f32[32,256]{1,0:T(8,128)} %get-tuple-element.40) | copy-start | bytes 98308
  187.5 4.8 %copy-start.13 = (f32[32,256]{1,0:T(8,128)S(1)}, f32[32,256]{1,0:T(8,128)}, u32[]{:S(2)}) copy-start(f32[32,256]{1,0:T(8,128)} %get-tuple-element.41) | copy-start | bytes 98308
  193.2 5.3 %collective-permute-start.2 = (f32[1,24,1,256]{3,2,1,0:T(1,128)S(1)}, f32[1,24,1,256]{3,2,1,0:T(1,128)S(1)}, u32[]{:S(2)}, u32[]{:S(2)}) collective-permute-start(f32[1,24,1,256]{3,2,1,0:T(1,128)S(1)} %get-tuple-element.27), channel_id=1, source_target_pairs={{0,8},{8,16},{16,24},{24,32},{32,40},{40,48},{48,56},{56,64},{64,7... | collective-permute-start | bytes 73736 | tf_op jit(solution)/shard_map/ppermute | solution.py:30
  195.9 6.7 %collective-permute-start.3 = (f32[1,24,1,256]{3,2,1,0:T(1,128)S(1)}, f32[1,24,1,256]{3,2,1,0:T(1,128)S(1)}, u32[]{:S(2)}, u32[]{:S(2)}) collective-permute-start(f32[1,24,1,256]{3,2,1,0:T(1,128)S(1)} %get-tuple-element.28), channel_id=1, source_target_pairs={{8,0},{16,8},{24,16},{32,24},{40,32},{48,40},{56,48},{64,56},{72,6... | collective-permute-start | bytes 73736 | tf_op jit(solution)/shard_map/ppermute | solution.py:31
  202.9 17.7 %collective-permute-start.4 = (f32[1,24,34,1]{3,2,1,0:T(8,128)S(1)}, f32[1,24,34,1]{3,2,1,0:T(8,128)S(1)}, u32[]{:S(2)}, u32[]{:S(2)}) collective-permute-start(f32[1,24,34,1]{3,2,1,0:T(8,128)S(1)} %get-tuple-element.11), channel_id=1, source_target_pairs={{0,1},{1,2},{2,3},{3,4},{4,5},{5,6},{6,7},{8,9},{9,10},{10,11},{11... | collective-permute-start | bytes 9800 | tf_op jit(solution)/shard_map/ppermute | solution.py:30
  214.7 28.9 %collective-permute-start.5 = (f32[1,24,34,1]{3,2,1,0:T(8,128)S(1)}, f32[1,24,34,1]{3,2,1,0:T(8,128)S(1)}, u32[]{:S(2)}, u32[]{:S(2)}) collective-permute-start(f32[1,24,34,1]{3,2,1,0:T(8,128)S(1)} %get-tuple-element.12), channel_id=1, source_target_pairs={{1,0},{2,1},{3,2},{4,3},{5,4},{6,5},{7,6},{9,8},{10,9},{11,10},{12... | collective-permute-start | bytes 9800 | tf_op jit(solution)/shard_map/ppermute | solution.py:31
  253.0 35.9 %collective-permute-start.7 = (f32[3,24,16,128]{3,2,1,0:T(8,128)}, f32[3,24,16,128]{3,2,1,0:T(8,128)}, u32[]{:S(2)}, u32[]{:S(2)}) collective-permute-start(f32[3,24,16,128]{3,2,1,0:T(8,128)} %pad_maximum_fusion.21), channel_id=1, source_target_pairs={{0,8},{8,0},{16,24},{24,16},{32,40},{40,32},{48,56},{56,48},{64,72... | collective-permute-start | bytes 1769480 | tf_op jit(solution)/shard_map/ppermute | solution.py:15
  262.1 26.8 %copy-start.1 = (f32[1,24,16,128]{3,2,1,0:T(8,128)S(1)}, f32[1,24,16,128]{3,2,1,0:T(8,128)}, u32[]{:S(2)}) copy-start(f32[1,24,16,128]{3,2,1,0:T(8,128)} %get-tuple-element.21) | copy-start | bytes 589828
  262.1 26.8 %copy-start.2 = (f32[1,24,16,128]{3,2,1,0:T(8,128)S(1)}, f32[1,24,16,128]{3,2,1,0:T(8,128)}, u32[]{:S(2)}) copy-start(f32[1,24,16,128]{3,2,1,0:T(8,128)} %get-tuple-element.25) | copy-start | bytes 589828
  277.5 13.4 %collective-permute-start.6 = (f32[3,24,16,128]{3,2,1,0:T(8,128)}, f32[3,24,16,128]{3,2,1,0:T(8,128)S(1)}, u32[]{:S(2)}, u32[]{:S(2)}) collective-permute-start(f32[3,24,16,128]{3,2,1,0:T(8,128)} %get-tuple-element.35), channel_id=1, source_target_pairs={{0,8},{8,0},{16,24},{24,16},{32,40},{40,32},{48,56},{56,48},{64,72... | collective-permute-start | bytes 1769480 | tf_op jit(solution)/shard_map/ppermute | solution.py:15
  353.9 6.4 %copy-start.4 = (f32[32,256]{1,0:T(8,128)S(1)}, f32[32,256]{1,0:T(8,128)}, u32[]{:S(2)}) copy-start(f32[32,256]{1,0:T(8,128)} %multiply_subtract_fusion) | copy-start | bytes 98308
  362.5 5.3 %collective-permute-start.8 = (f32[1,24,1,256]{3,2,1,0:T(1,128)S(1)}, f32[1,24,1,256]{3,2,1,0:T(1,128)S(1)}, u32[]{:S(2)}, u32[]{:S(2)}) collective-permute-start(f32[1,24,1,256]{3,2,1,0:T(1,128)S(1)} %get-tuple-element.19), channel_id=1, source_target_pairs={{0,8},{8,16},{16,24},{24,32},{32,40},{40,48},{48,56},{56,64},{64,7... | collective-permute-start | bytes 73736 | tf_op jit(solution)/shard_map/ppermute | solution.py:30
  365.6 6.7 %collective-permute-start.9 = (f32[1,24,1,256]{3,2,1,0:T(1,128)S(1)}, f32[1,24,1,256]{3,2,1,0:T(1,128)S(1)}, u32[]{:S(2)}, u32[]{:S(2)}) collective-permute-start(f32[1,24,1,256]{3,2,1,0:T(1,128)S(1)} %get-tuple-element.20), channel_id=1, source_target_pairs={{8,0},{16,8},{24,16},{32,24},{40,32},{48,40},{56,48},{64,56},{72,6... | collective-permute-start | bytes 73736 | tf_op jit(solution)/shard_map/ppermute | solution.py:31
  372.6 17.6 %collective-permute-start.10 = (f32[1,24,34,1]{3,2,1,0:T(8,128)S(1)}, f32[1,24,34,1]{3,2,1,0:T(8,128)S(1)}, u32[]{:S(2)}, u32[]{:S(2)}) collective-permute-start(f32[1,24,34,1]{3,2,1,0:T(8,128)S(1)} %get-tuple-element.9), channel_id=1, source_target_pairs={{0,1},{1,2},{2,3},{3,4},{4,5},{5,6},{6,7},{8,9},{9,10},{10,11},{11... | collective-permute-start | bytes 9800 | tf_op jit(solution)/shard_map/ppermute | solution.py:30
  384.3 28.7 %collective-permute-start.11 = (f32[1,24,34,1]{3,2,1,0:T(8,128)S(1)}, f32[1,24,34,1]{3,2,1,0:T(8,128)S(1)}, u32[]{:S(2)}, u32[]{:S(2)}) collective-permute-start(f32[1,24,34,1]{3,2,1,0:T(8,128)S(1)} %get-tuple-element.10), channel_id=1, source_target_pairs={{1,0},{2,1},{3,2},{4,3},{5,4},{6,5},{7,6},{9,8},{10,9},{11,10},{12... | collective-permute-start | bytes 9800 | tf_op jit(solution)/shard_map/ppermute | solution.py:31
  (8 other events, 28.9 us)
Sparse Core Ops, SparseCore 0:
  114.6 66.8 all-reduce.4
  291.1 60.0 all-reduce.6
where the time goes:
time: 424 us; the launch traced here: 422 us
  local copies, waits for them, and re-layouts  133 us (31%)
  waiting for transfers between devices  96.1 us (23%)
  other arithmetic  69.2 us (16%)
  starting transfers between devices  48.6 us (11%)
  between operations  44.1 us (10%)
  blocking collectives  30.5 us (7%)
    dynamic_update_slice x12, local copies, waits for them, and re-layouts, local(): lax.dynamic_update_slice(gathered, existing + pieces[slot], (anchor, tops...  101 us
    ppermute x4, waiting for transfers between devices, padded_2(): after = lax.ppermute(leading, axis, down)  54.4 us
    psum x2, waiting for transfers between devices, spread(): return lax.psum(block, axis)  33.9 us
    all_gather x2, blocking collectives, local(): lax.all_gather(child_block[None], 'grid', axis=0, tiled=True)[1:]  30.5 us
    ppermute x4, starting transfers between devices, padded_2(): before = lax.ppermute(last, axis, up)  29.3 us
    reduce_sum x2, other arithmetic, block_sums(): values.reshape(shape[:-2] + (shape[-2] // 2, 2, shape[-1] // 2, 2))  14.3 us
    mul x2, other arithmetic, local(): keep_here[slot]  12.3 us
    ppermute x4, starting transfers between devices, partner(): return lax.ppermute(value, axis, pairs)  10.5 us
  transfers between devices with their start and end apart: 14, of which 8 were waited for; matrix products, arithmetic and copies ran while one was open for 37% of the time, Pallas kernels for 0%

commit v1 on v0

--- a/solution.py
+++ b/solution.py
@@ -142,7 +142,10 @@
                 for slot in range(slots)
             ]
         )
-        gathered_up = lax.all_gather(child_block[None], "grid", axis=0, tiled=True)[1:]
+        gathered_up = jnp.concatenate(
+            lax.all_to_all(jnp.stack([child_block[None]] * lax.axis_size("grid")), "grid", 0, 0),
+            axis=0,
+        )[1:]
         up_keep = keep_here[:, None, None, None] * gathered_up
         up_send = (1.0 - keep_here)[:, None, None, None] * gathered_up
         up_cross, down_cross = partner((up_send, down_there), "gx", 0)

time: 424 us -> 494 us (1.17)
  waiting for transfers between devices: 96.1 us -> 181 us
  blocking collectives: 30.5 us -> 0 us
  starting transfers between devices: 48.6 us -> 56.7 us
    psum x2, waiting for transfers between devices: 33.9 us -> 117 us  [spread(): return lax.psum(block, axis)]
    all_gather x2 -> x0, blocking collectives: 30.5 us -> none  [local(): lax.all_gather(child_block[None], 'grid', axis=0, tiled=True)[1:]]
    all_to_all x0 -> x2, starting transfers between devices: none -> 9.11 us  [local(): lax.all_to_all(jnp.stack([child_block[None]] * lax.axis_size('grid')), 'g...]
    ppermute x4, waiting for transfers between devices: 0.01 us -> 8.71 us  [partner(): return lax.ppermute(value, axis, pairs)]
    ppermute x4, waiting for transfers between devices: 54.4 us -> 49.4 us  [padded_2(): after = lax.ppermute(leading, axis, down)]
  transfers between devices with their start and end apart: 14 -> 16, of which waited for: 8 -> 9; matrix products, arithmetic and copies ran while one was open for 37% -> 17% of each run, Pallas kernels for 0% -> 0%
where the time goes in v1:
time: 494 us; the launch traced here: 492 us
  waiting for transfers between devices  181 us (37%)
  local copies, waits for them, and re-layouts  137 us (28%)
  other arithmetic  73.5 us (15%)
  starting transfers between devices  56.7 us (11%)
  between operations  43.9 us (9%)
    psum x2, waiting for transfers between devices, spread(): return lax.psum(block, axis)  117 us
    dynamic_update_slice x12, local copies, waits for them, and re-layouts, local(): lax.dynamic_update_slice(gathered, existing + pieces[slot], (anchor, tops...  101 us
    ppermute x4, waiting for transfers between devices, padded_2(): after = lax.ppermute(leading, axis, down)  49.4 us
    ppermute x4, starting transfers between devices, padded_2(): before = lax.ppermute(last, axis, up)  30.4 us
    reduce_sum x2, other arithmetic, block_sums(): values.reshape(shape[:-2] + (shape[-2] // 2, 2, shape[-1] // 2, 2))  14.3 us
    add x10, other arithmetic, local(): existing + pieces[slot]  12.4 us
    mul x2, other arithmetic, local(): keep_here[slot]  11 us
  transfers between devices with their start and end apart: 16, of which 9 were waited for; matrix products, arithmetic and copies ran while one was open for 17% of the time, Pallas kernels for 0%

profile of v1, /device:TPU:25, one launch (start us, length us, event | category | flops | bytes accessed | tf_op | source)
XLA Modules:
  0.0 491.8 jit_solution(3352885508497029369)
XLA Ops:
  33.3 6.6 %dynamic-slice_multiply_fusion.11 = (f32[1,24,16,128]{3,2,1,0:T(8,128)S(1)}, f32[1,24,16,128]{3,2,1,0:T(8,128)S(1)}, f32[1,24,16,128]{3,2,1,0:T(8,128)S(1)}, f32...) fusion(f32[1,24,32,256]{3,2,1,0:T(8,128)} %param.10, s32[]{:T(128)S(6)} %select_n.61, ...), kind=kLoop, calls=%fused_computation.91 | loop fusion | flops 294912 | bytes 2359368 | tf_op jit(solution)/shard_map/mul | solution.py:125
  47.9 7.2 %multiply_reduce_fusion.1 = f32[24,16,128]{0,2,1:T(8,128)} fusion(f32[24,16,2,128,2]{0,4,3,2,1:T(2,128)} %bitcast.127, f32[16,2,128,2]{3,2,1,0:T(8,128)S(1)} %mul.540), kind=kLoop, calls=%fused_computation.1 | loop fusion | flops 344064 | bytes 1015808 | tf_op jit(solution)/shard_map/reduce_sum | solution.py:38
  59.2 5.6 %all-to-all-start = ((f32[4,1,24,16,128]{4,3,2,1,0:T(8,128)}), f32[4,1,24,16,128]{4,3,2,1,0:T(8,128)}, u32[]{:S(2)}, u32[]{:S(2)}) async-start(f32[4,1,24,16,128]{4,3,2,1,0:T(8,128)} %stack.16), calls=%async_computation | async-start | bytes 1572864 | tf_op jit(solution)/shard_map/all_to_all | solution.py:146
  82.0 4.7 multiply_subtract_fusion
  97.2 58.3 %all-reduce.5.cloned.1.call-done = f32[3,24,16,128]{3,2,1,0:T(8,128)} async-done(((f32[3,24,16,128]{3,2,1,0:T(8,128)}), f32[3,24,16,128]{3,2,1,0:T(8,128)}) %all-reduce.5.cloned.1.call-update) | async-done | bytes 589840 | tf_op jit(solution)/shard_map/psum | solution.py:20
  167.9 9.0 %dynamic_update_slice.36 = f32[24,32,256]{2,1,0:T(8,128)} dynamic-update-slice(f32[24,32,256]{2,1,0:T(8,128)} %broadcast.567.clone, f32[24,16,128]{2,1,0:T(8,128)} %slice_bitcast_fusion.13, s32[]{:T(128)} %constant.55.clone.1, s32[]{:T(128)S(6)} %select_n.61, s32[]{:T(128)S(6)} %select_n.62) | dynamic-update-slice | bytes 393220 | tf_op jit(solution)/shard_map/dynamic_update_slice | solution.py:164
  178.9 9.0 %dynamic_update_slice.37 = f32[24,32,256]{2,1,0:T(8,128)} dynamic-update-slice(f32[24,32,256]{2,1,0:T(8,128)} %dynamic_update_slice.36, f32[24,16,128]{2,1,0:T(8,128)} %fusion.31, s32[]{:T(128)} %constant.55.clone.1, s32[]{:T(128)S(6)} %select_n.63, s32[]{:T(128)S(6)} %select_n.64) | dynamic-update-slice | bytes 393220 | tf_op jit(solution)/shard_map/dynamic_update_slice | solution.py:164
  189.7 8.4 %dynamic_update_slice.38 = f32[24,32,256]{2,1,0:T(8,128)} dynamic-update-slice(f32[24,32,256]{2,1,0:T(8,128)} %dynamic_update_slice.37, f32[24,16,128]{2,1,0:T(8,128)} %fusion.30, s32[]{:T(128)} %constant.55.clone.1, s32[]{:T(128)S(6)} %select_n.65, s32[]{:T(128)S(6)} %select_n.66) | dynamic-update-slice | bytes 393220 | tf_op jit(solution)/shard_map/dynamic_update_slice | solution.py:164
  200.1 9.0 %dynamic_update_slice.39 = f32[24,32,256]{2,1,0:T(8,128)} dynamic-update-slice(f32[24,32,256]{2,1,0:T(8,128)} %dynamic_update_slice.38, f32[24,16,128]{2,1,0:T(8,128)} %fusion.29, s32[]{:T(128)} %constant.55.clone.1, s32[]{:T(128)S(6)} %select_n.67, s32[]{:T(128)S(6)} %select_n.68) | dynamic-update-slice | bytes 393220 | tf_op jit(solution)/shard_map/dynamic_update_slice | solution.py:164
  211.0 9.1 %dynamic_update_slice.40 = f32[24,32,256]{2,1,0:T(8,128)} dynamic-update-slice(f32[24,32,256]{2,1,0:T(8,128)} %dynamic_update_slice.39, f32[24,16,128]{2,1,0:T(8,128)} %fusion.28, s32[]{:T(128)} %constant.55.clone.1, s32[]{:T(128)S(6)} %select_n.69, s32[]{:T(128)S(6)} %select_n.70) | dynamic-update-slice | bytes 393220 | tf_op jit(solution)/shard_map/dynamic_update_slice | solution.py:164
  221.4 9.0 %dynamic_update_slice.41 = f32[24,32,256]{2,1,0:T(8,128)} dynamic-update-slice(f32[24,32,256]{2,1,0:T(8,128)} %dynamic_update_slice.40, f32[24,16,128]{2,1,0:T(8,128)S(1)} %fusion.27, s32[]{:T(128)} %constant.55.clone.1, s32[]{:T(128)S(6)} %select_n.71, s32[]{:T(128)S(6)} %select_n.72) | dynamic-update-slice | bytes 393220 | tf_op jit(solution)/shard_map/dynamic_update_slice | solution.py:164
  243.5 11.7 %collective-permute-start.4 = (f32[1,24,34,1]{3,1,2,0:T(8,128)S(1)}, f32[1,24,34,1]{3,1,2,0:T(8,128)S(1)}, u32[]{:S(2)}, u32[]{:S(2)}) collective-permute-start(f32[1,24,34,1]{3,1,2,0:T(8,128)S(1)} %get-tuple-element.15), channel_id=1, source_target_pairs={{0,1},{1,2},{2,3},{3,4},{4,5},{5,6},{6,7},{8,9},{9,10},{10,11},{11... | collective-permute-start | bytes 9800 | tf_op jit(solution)/shard_map/ppermute | solution.py:30
  260.4 20.6 %collective-permute-done.5 = f32[1,24,34,1]{3,1,2,0:T(8,128)S(1)} collective-permute-done((f32[1,24,34,1]{3,1,2,0:T(8,128)S(1)}, f32[1,24,34,1]{3,1,2,0:T(8,128)S(1)}, u32[]{:S(2)}, u32[]{:S(2)}) %collective-permute-start.5) | collective-permute-done | bytes 3296 | tf_op jit(solution)/shard_map/ppermute | solution.py:31
  285.0 7.1 %multiply_reduce_fusion = f32[24,16,128]{0,2,1:T(8,128)} fusion(f32[24,16,2,128,2]{0,4,3,2,1:T(2,128)} %bitcast.128, f32[16,2,128,2]{3,2,1,0:T(8,128)S(1)} %mul.540), kind=kLoop, calls=%fused_computation | loop fusion | flops 344064 | bytes 1015808 | tf_op jit(solution)/shard_map/reduce_sum | solution.py:38
  304.5 8.7 %collective-permute-done.7 = f32[3,24,16,128]{3,2,1,0:T(8,128)S(1)} collective-permute-done((f32[3,24,16,128]{3,2,1,0:T(8,128)S(1)}, f32[3,24,16,128]{3,2,1,0:T(8,128)S(1)}, u32[]{:S(2)}, u32[]{:S(2)}) %collective-permute-start.7) | collective-permute-done | bytes 589856 | tf_op jit(solution)/shard_map/ppermute | solution.py:15
  317.1 58.5 %all-reduce.7.cloned.1.call-done = f32[3,24,16,128]{3,2,1,0:T(8,128)} async-done(((f32[3,24,16,128]{3,2,1,0:T(8,128)}), f32[3,24,16,128]{3,2,1,0:T(8,128)}) %all-reduce.7.cloned.1.call-update) | async-done | bytes 589840 | tf_op jit(solution)/shard_map/psum | solution.py:20
  382.3 7.9 %dynamic_update_slice.42 = f32[24,32,256]{2,1,0:T(8,128)S(1)} dynamic-update-slice(f32[24,32,256]{2,1,0:T(8,128)S(1)} %broadcast.567, f32[24,16,128]{2,1,0:T(8,128)S(1)} %slice_bitcast_fusion.7, s32[]{:T(128)} %constant.55.clone.1, s32[]{:T(128)S(6)} %select_n.61, s32[]{:T(128)S(6)} %select_n.62) | dynamic-update-slice | bytes 393220 | tf_op jit(solution)/shard_map/dynamic_update_slice | solution.py:164
  391.3 7.9 %dynamic_update_slice.43 = f32[24,32,256]{2,1,0:T(8,128)S(1)} dynamic-update-slice(f32[24,32,256]{2,1,0:T(8,128)S(1)} %dynamic_update_slice.42, f32[24,16,128]{2,1,0:T(8,128)S(1)} %fusion.26, s32[]{:T(128)} %constant.55.clone.1, s32[]{:T(128)S(6)} %select_n.63, s32[]{:T(128)S(6)} %select_n.64) | dynamic-update-slice | bytes 393220 | tf_op jit(solution)/shard_map/dynamic_update_slice | solution.py:164
  399.3 7.7 %dynamic_update_slice.44 = f32[24,32,256]{2,1,0:T(8,128)S(1)} dynamic-update-slice(f32[24,32,256]{2,1,0:T(8,128)S(1)} %dynamic_update_slice.43, f32[24,16,128]{2,1,0:T(8,128)S(1)} %fusion.25, s32[]{:T(128)} %constant.55.clone.1, s32[]{:T(128)S(6)} %select_n.65, s32[]{:T(128)S(6)} %select_n.66) | dynamic-update-slice | bytes 393220 | tf_op jit(solution)/shard_map/dynamic_update_slice | solution.py:164
  408.1 7.9 %dynamic_update_slice.45 = f32[24,32,256]{2,1,0:T(8,128)S(1)} dynamic-update-slice(f32[24,32,256]{2,1,0:T(8,128)S(1)} %dynamic_update_slice.44, f32[24,16,128]{2,1,0:T(8,128)S(1)} %fusion.24, s32[]{:T(128)} %constant.55.clone.1, s32[]{:T(128)S(6)} %select_n.67, s32[]{:T(128)S(6)} %select_n.68) | dynamic-update-slice | bytes 393220 | tf_op jit(solution)/shard_map/dynamic_update_slice | solution.py:164
  416.1 7.9 %dynamic_update_slice.46 = f32[24,32,256]{2,1,0:T(8,128)S(1)} dynamic-update-slice(f32[24,32,256]{2,1,0:T(8,128)S(1)} %dynamic_update_slice.45, f32[24,16,128]{2,1,0:T(8,128)S(1)} %fusion.23, s32[]{:T(128)} %constant.55.clone.1, s32[]{:T(128)S(6)} %select_n.69, s32[]{:T(128)S(6)} %select_n.70) | dynamic-update-slice | bytes 393220 | tf_op jit(solution)/shard_map/dynamic_update_slice | solution.py:164
  425.1 7.9 %dynamic_update_slice.47 = f32[24,32,256]{2,1,0:T(8,128)S(1)} dynamic-update-slice(f32[24,32,256]{2,1,0:T(8,128)S(1)} %dynamic_update_slice.46, f32[24,16,128]{2,1,0:T(8,128)S(1)} %fusion.22, s32[]{:T(128)} %constant.55.clone.1, s32[]{:T(128)S(6)} %select_n.71, s32[]{:T(128)S(6)} %select_n.72) | dynamic-update-slice | bytes 393220 | tf_op jit(solution)/shard_map/dynamic_update_slice | solution.py:164
  445.4 11.8 %collective-permute-start.10 = (f32[1,24,34,1]{3,1,2,0:T(8,128)S(1)}, f32[1,24,34,1]{3,1,2,0:T(8,128)S(1)}, u32[]{:S(2)}, u32[]{:S(2)}) collective-permute-start(f32[1,24,34,1]{3,1,2,0:T(8,128)S(1)} %get-tuple-element.11), channel_id=1, source_target_pairs={{0,1},{1,2},{2,3},{3,4},{4,5},{5,6},{6,7},{8,9},{9,10},{10,11},{11... | collective-permute-start | bytes 9800 | tf_op jit(solution)/shard_map/ppermute | solution.py:30
  462.3 20.4 %collective-permute-done.11 = f32[1,24,34,1]{3,1,2,0:T(8,128)S(1)} collective-permute-done((f32[1,24,34,1]{3,1,2,0:T(8,128)S(1)}, f32[1,24,34,1]{3,1,2,0:T(8,128)S(1)}, u32[]{:S(2)}, u32[]{:S(2)}) %collective-permute-start.11) | collective-permute-done | bytes 3296 | tf_op jit(solution)/shard_map/ppermute | solution.py:31
  (158 shorter events, 126.0 us)
Async XLA Ops:
  6.5 36.6 %copy-start = (f32[1,24,32,256]{3,2,1,0:T(8,128)S(1)}, f32[1,24,32,256]{3,2,1,0:T(8,128)}, u32[]{:S(2)}) copy-start(f32[1,24,32,256]{3,2,1,0:T(8,128)} %param.10) | copy-start | bytes 2359300
  40.8 47.3 %collective-permute-start.1 = (f32[3,24,16,128]{3,2,1,0:T(8,128)}, f32[3,24,16,128]{3,2,1,0:T(8,128)}, u32[]{:S(2)}, u32[]{:S(2)}) collective-permute-start(f32[3,24,16,128]{3,2,1,0:T(8,128)} %pad_maximum_fusion.10), channel_id=1, source_target_pairs={{0,8},{8,0},{16,24},{24,16},{32,40},{40,32},{48,56},{56,48},{64,72... | collective-permute-start | bytes 1769480 | tf_op jit(solution)/shard_map/ppermute | solution.py:15
  59.2 31.0 %all-to-all-start = ((f32[4,1,24,16,128]{4,3,2,1,0:T(8,128)}), f32[4,1,24,16,128]{4,3,2,1,0:T(8,128)}, u32[]{:S(2)}, u32[]{:S(2)}) async-start(f32[4,1,24,16,128]{4,3,2,1,0:T(8,128)} %stack.16), calls=%async_computation | async-start | bytes 1572864 | tf_op jit(solution)/shard_map/all_to_all | solution.py:146
  64.8 90.7 %all-reduce.5.cloned.1.call-start = ((), (), s32[]{:S(2)}) async-start(), calls=%async_computation.2 | async-start | bytes 1179648 | tf_op jit(solution)/shard_map/psum | solution.py:20
  92.2 84.7 %collective-permute-start = (f32[3,24,16,128]{3,2,1,0:T(8,128)}, f32[3,24,16,128]{3,2,1,0:T(8,128)}, u32[]{:S(2)}, u32[]{:S(2)}) collective-permute-start(f32[3,24,16,128]{3,2,1,0:T(8,128)} %get-tuple-element.41), channel_id=1, source_target_pairs={{0,8},{8,0},{16,24},{24,16},{32,40},{40,32},{48,56},{56,48},{64,72... | collective-permute-start | bytes 1769480 | tf_op jit(solution)/shard_map/ppermute | solution.py:15
  211.0 21.0 %copy-start.10 = (f32[32,256]{1,0:T(8,128)S(1)}, f32[32,256]{1,0:T(8,128)}, u32[]{:S(2)}) copy-start(f32[32,256]{1,0:T(8,128)} %get-tuple-element.45) | copy-start | bytes 98308
  232.9 5.7 %collective-permute-start.2 = (f32[1,24,1,256]{3,1,2,0:T(8,128)S(1)}, f32[1,24,1,256]{3,1,2,0:T(8,128)S(1)}, u32[]{:S(2)}, u32[]{:S(2)}) collective-permute-start(f32[1,24,1,256]{3,1,2,0:T(8,128)S(1)} %copy.191), channel_id=1, source_target_pairs={{0,8},{8,16},{16,24},{24,32},{32,40},{40,48},{48,56},{56,64},{64,7... | collective-permute-start | bytes 73736 | tf_op jit(solution)/shard_map/ppermute | solution.py:30
  236.6 6.7 %collective-permute-start.3 = (f32[1,24,1,256]{3,1,2,0:T(8,128)S(1)}, f32[1,24,1,256]{3,1,2,0:T(8,128)S(1)}, u32[]{:S(2)}, u32[]{:S(2)}) collective-permute-start(f32[1,24,1,256]{3,1,2,0:T(8,128)S(1)} %copy.193), channel_id=1, source_target_pairs={{8,0},{16,8},{24,16},{32,24},{40,32},{48,40},{56,48},{64,56},{72,6... | collective-permute-start | bytes 73736 | tf_op jit(solution)/shard_map/ppermute | solution.py:31
  243.5 16.9 %collective-permute-start.4 = (f32[1,24,34,1]{3,1,2,0:T(8,128)S(1)}, f32[1,24,34,1]{3,1,2,0:T(8,128)S(1)}, u32[]{:S(2)}, u32[]{:S(2)}) collective-permute-start(f32[1,24,34,1]{3,1,2,0:T(8,128)S(1)} %get-tuple-element.15), channel_id=1, source_target_pairs={{0,1},{1,2},{2,3},{3,4},{4,5},{5,6},{6,7},{8,9},{9,10},{10,11},{11... | collective-permute-start | bytes 9800 | tf_op jit(solution)/shard_map/ppermute | solution.py:30
  255.2 25.7 %collective-permute-start.5 = (f32[1,24,34,1]{3,1,2,0:T(8,128)S(1)}, f32[1,24,34,1]{3,1,2,0:T(8,128)S(1)}, u32[]{:S(2)}, u32[]{:S(2)}) collective-permute-start(f32[1,24,34,1]{3,1,2,0:T(8,128)S(1)} %get-tuple-element.16), channel_id=1, source_target_pairs={{1,0},{2,1},{3,2},{4,3},{5,4},{6,5},{7,6},{9,8},{10,9},{11,10},{12... | collective-permute-start | bytes 9800 | tf_op jit(solution)/shard_map/ppermute | solution.py:31
  294.6 19.6 %all-to-all-start.1 = ((f32[4,1,24,16,128]{4,3,2,1,0:T(8,128)}), f32[4,1,24,16,128]{4,3,2,1,0:T(8,128)S(1)}, u32[]{:S(2)}, u32[]{:S(2)}) async-start(f32[4,1,24,16,128]{4,3,2,1,0:T(8,128)} %stack.20), calls=%async_computation.1 | async-start | bytes 1572864 | tf_op jit(solution)/shard_map/all_to_all | solution.py:146
  298.1 77.5 %all-reduce.7.cloned.1.call-start = ((), (), s32[]{:S(2)}) async-start(), calls=%async_computation.3 | async-start | bytes 1179648 | tf_op jit(solution)/shard_map/psum | solution.py:20
  302.6 10.6 %collective-permute-start.7 = (f32[3,24,16,128]{3,2,1,0:T(8,128)S(1)}, f32[3,24,16,128]{3,2,1,0:T(8,128)S(1)}, u32[]{:S(2)}, u32[]{:S(2)}) collective-permute-start(f32[3,24,16,128]{3,2,1,0:T(8,128)S(1)} %pad_maximum_fusion.11), channel_id=1, source_target_pairs={{0,8},{8,0},{16,24},{24,16},{32,40},{40,32},{48,56},{56,48},{64,72... | collective-permute-start | bytes 1769480 | tf_op jit(solution)/shard_map/ppermute | solution.py:15
  315.2 75.1 %collective-permute-start.6 = (f32[3,24,16,128]{3,2,1,0:T(8,128)}, f32[3,24,16,128]{3,2,1,0:T(8,128)}, u32[]{:S(2)}, u32[]{:S(2)}) collective-permute-start(f32[3,24,16,128]{3,2,1,0:T(8,128)} %get-tuple-element.31), channel_id=1, source_target_pairs={{0,8},{8,0},{16,24},{24,16},{32,40},{40,32},{48,56},{56,48},{64,72... | collective-permute-start | bytes 1769480 | tf_op jit(solution)/shard_map/ppermute | solution.py:15
  382.1 50.9 %copy-start.1 = (f32[32,256]{1,0:T(8,128)S(1)}, f32[32,256]{1,0:T(8,128)}, u32[]{:S(2)}) copy-start(f32[32,256]{1,0:T(8,128)} %subtract_bitcast_fusion) | copy-start | bytes 98308
  382.2 52.2 %copy-start.3 = (f32[1,32,256]{2,1,0:T(8,128)S(1)}, f32[1,32,256]{2,1,0:T(8,128)}, u32[]{:S(2)}) copy-start(f32[1,32,256]{2,1,0:T(8,128)} %param.13) | copy-start | bytes 98308
  382.3 52.2 %copy-start.5 = (f32[1,32,256]{2,1,0:T(8,128)S(1)}, f32[1,32,256]{2,1,0:T(8,128)}, u32[]{:S(2)}) copy-start(f32[1,32,256]{2,1,0:T(8,128)} %param.14) | copy-start | bytes 98308
  382.3 52.2 %copy-start.7 = (f32[32,256]{1,0:T(8,128)S(1)}, f32[32,256]{1,0:T(8,128)}, u32[]{:S(2)}) copy-start(f32[32,256]{1,0:T(8,128)} %get-tuple-element.43) | copy-start | bytes 98308
  382.3 52.2 %copy-start.9 = (f32[32,256]{1,0:T(8,128)S(1)}, f32[32,256]{1,0:T(8,128)}, u32[]{:S(2)}) copy-start(f32[32,256]{1,0:T(8,128)} %get-tuple-element.44) | copy-start | bytes 98308
  382.3 52.2 %copy-start.11 = (f32[32,256]{1,0:T(8,128)S(1)}, f32[32,256]{1,0:T(8,128)}, u32[]{:S(2)}) copy-start(f32[32,256]{1,0:T(8,128)} %get-tuple-element.45) | copy-start | bytes 98308
  435.3 5.3 %collective-permute-start.8 = (f32[1,24,1,256]{3,1,2,0:T(8,128)S(1)}, f32[1,24,1,256]{3,1,2,0:T(8,128)S(1)}, u32[]{:S(2)}, u32[]{:S(2)}) collective-permute-start(f32[1,24,1,256]{3,1,2,0:T(8,128)S(1)} %copy.204), channel_id=1, source_target_pairs={{0,8},{8,16},{16,24},{24,32},{32,40},{40,48},{48,56},{56,64},{64,7... | collective-permute-start | bytes 73736 | tf_op jit(solution)/shard_map/ppermute | solution.py:30
  438.6 6.7 %collective-permute-start.9 = (f32[1,24,1,256]{3,1,2,0:T(8,128)S(1)}, f32[1,24,1,256]{3,1,2,0:T(8,128)S(1)}, u32[]{:S(2)}, u32[]{:S(2)}) collective-permute-start(f32[1,24,1,256]{3,1,2,0:T(8,128)S(1)} %copy.206), channel_id=1, source_target_pairs={{8,0},{16,8},{24,16},{32,24},{40,32},{48,40},{56,48},{64,56},{72,6... | collective-permute-start | bytes 73736 | tf_op jit(solution)/shard_map/ppermute | solution.py:31
  445.4 16.9 %collective-permute-start.10 = (f32[1,24,34,1]{3,1,2,0:T(8,128)S(1)}, f32[1,24,34,1]{3,1,2,0:T(8,128)S(1)}, u32[]{:S(2)}, u32[]{:S(2)}) collective-permute-start(f32[1,24,34,1]{3,1,2,0:T(8,128)S(1)} %get-tuple-element.11), channel_id=1, source_target_pairs={{0,1},{1,2},{2,3},{3,4},{4,5},{5,6},{6,7},{8,9},{9,10},{10,11},{11... | collective-permute-start | bytes 9800 | tf_op jit(solution)/shard_map/ppermute | solution.py:30
  457.2 25.6 %collective-permute-start.11 = (f32[1,24,34,1]{3,1,2,0:T(8,128)S(1)}, f32[1,24,34,1]{3,1,2,0:T(8,128)S(1)}, u32[]{:S(2)}, u32[]{:S(2)}) collective-permute-start(f32[1,24,34,1]{3,1,2,0:T(8,128)S(1)} %get-tuple-element.12), channel_id=1, source_target_pairs={{1,0},{2,1},{3,2},{4,3},{5,4},{6,5},{7,6},{9,8},{10,9},{11,10},{12... | collective-permute-start | bytes 9800 | tf_op jit(solution)/shard_map/ppermute | solution.py:31
  (7 other events, 98.2 us)
Sparse Core Ops, SparseCore 0:
  90.2 65.2 all-reduce.4
  314.3 61.2 all-reduce.6
